TPU v7x, 256 devices: a whole 4x4x8 slice. The times are simulated.
256 devices in a mesh: list: 32 (over x, y, core), rep: 8 (over z).
Axes of the slice: x: 4, y: 4, z: 8, core: 2. Of those that a mesh axis runs over, the one named last changes fastest.
Arguments:
- memory_rows: bfloat16 [65536, 1024], P(('list', 'rep'))
- list_owner: int32 [65536, 1], P(('list', 'rep')), may hold values from 0 to 31; in each aligned block of 256 rows (0 to 255, 256 to 511, ...) at most 32 rows name the same one
- list_slot: int32 [65536], P(('list', 'rep')), may hold values from 0 to 2047
- pq_codes: int32 [65536, 16], P(('list', 'rep')), may hold values from 0 to 255
- valid_rows: int32 [256], P(('list', 'rep')), may hold values from 128 to 256
- centroids: bfloat16 [65536, 1024], P('list'), may hold values from -3 to 3
- codebook: float32 [16, 256, 64], replicated
Outputs:
- new_codebook: float32 [16, 256, 64], P('rep')
- row_error: float32 [65536], P(('list', 'rep'))
Inputs may be any that keep to these rules, and one draw needn't show every extreme that they name: `list_owner`: the rows of one device name one index of list at most 32 times, and some device's rows name one exactly 32 times.
All inputs are finite; a program needn't handle non-finite values.
Results may differ from a plain program's by a relative error of at most 0.0038.
Values may be sent and summed in bfloat16 or wider, within the bound.
A program may use at most 128 MiB of HBM per device.

v0:
```python
import jax
import jax.numpy as jnp
from jax import lax
from jax.sharding import PartitionSpec as P

prior_weight = 4.0


def code_statistics(residual, pq_codes, is_live, codebook):
    row_count = residual.shape[0]
    subspaces = codebook.shape[0]
    code_count = codebook.shape[1]
    width_sub = codebook.shape[2]
    residual = jnp.where(is_live[:, None], residual, 0.0)
    recon = codebook[jnp.arange(subspaces)[None, :], pq_codes].reshape(
        row_count, subspaces * width_sub
    )
    row_error = jnp.where(is_live, jnp.mean((residual - recon) ** 2, axis=1), 0.0)
    rounded = (
        residual.astype(jnp.bfloat16).reshape(row_count, subspaces, width_sub).transpose(1, 0, 2)
    )
    codes_major = pq_codes.T

    def per_subspace(item):
        code_col, part_rows = item
        onehot = ((code_col[:, None] == jnp.arange(code_count)[None, :]) & is_live[:, None]).astype(
            jnp.bfloat16
        )
        sums_one = lax.dot_general(
            onehot, part_rows, (((0,), (0,)), ((), ())), preferred_element_type=jnp.float32
        )
        counts_one = jnp.sum(onehot.astype(jnp.float32), axis=0)
        return (sums_one, counts_one)

    sums, counts = lax.map(per_subspace, (codes_major, rounded))
    return (row_error, sums, counts)


def body(memory_rows, list_owner, list_slot, pq_codes, valid_rows, centroids, codebook):
    row_count = memory_rows.shape[0]
    width = memory_rows.shape[1]
    list_count = centroids.shape[0]
    owners = lax.axis_size("list")
    capacity = 4 * row_count // owners
    is_valid = jnp.arange(row_count) < valid_rows[0]
    target = list_owner[:, 0]
    onehot_dest = ((target[:, None] == jnp.arange(owners)[None, :]) & is_valid[:, None]).astype(
        jnp.int32
    )
    before = jnp.cumsum(onehot_dest, axis=0) - onehot_dest
    slot_rank = jnp.sum(before * onehot_dest, axis=1)
    position = jnp.where(is_valid, target * capacity + slot_rank, owners * capacity)
    taken = jnp.clip(position, 0, owners * capacity - 1)
    total_slots = owners * capacity
    send_rows = (
        jnp.zeros((total_slots, width), jnp.bfloat16).at[position].set(memory_rows, mode="drop")
    )
    send_slot = jnp.full((total_slots,), -1, jnp.int32).at[position].set(list_slot, mode="drop")
    send_codes = (
        jnp.zeros((total_slots, pq_codes.shape[1]), jnp.int32)
        .at[position]
        .set(pq_codes, mode="drop")
    )
    got_rows, got_slot, got_codes = (
        lax.all_to_all(
            send_rows.reshape(owners, capacity, width),
            "list",
            split_axis=0,
            concat_axis=0,
            tiled=True,
        ),
        lax.all_to_all(
            send_slot.reshape(owners, capacity), "list", split_axis=0, concat_axis=0, tiled=True
        ),
        lax.all_to_all(
            send_codes.reshape(owners, capacity, pq_codes.shape[1]),
            "list",
            split_axis=0,
            concat_axis=0,
            tiled=True,
        ),
    )
    got_rows = got_rows.reshape(total_slots, width)
    got_slot = got_slot.reshape(total_slots)
    got_codes = got_codes.reshape(total_slots, pq_codes.shape[1])
    is_live = got_slot >= 0
    centre = centroids[jnp.clip(got_slot, 0, list_count - 1)].astype(jnp.float32)
    residual = got_rows.astype(jnp.float32) - centre
    slot_error, sums, counts = code_statistics(residual, got_codes, is_live, codebook)
    returned = lax.all_to_all(
        slot_error.reshape(owners, capacity), "list", split_axis=0, concat_axis=0, tiled=True
    )
    row_error = jnp.where(is_valid, returned.reshape(total_slots)[taken], 0.0)
    subspaces = codebook.shape[0]
    replicas = lax.axis_size("rep")
    share = subspaces // replicas
    first_sub = lax.axis_index("rep") * share
    sums_all, counts_all = lax.psum((sums, counts), ("list", "rep"))
    sums_mine = lax.dynamic_slice_in_dim(sums_all, first_sub, share, 0)
    counts_mine = lax.dynamic_slice_in_dim(counts_all, first_sub, share, 0)
    old_mine = lax.dynamic_slice_in_dim(codebook, first_sub, share, 0)
    new_codebook = (sums_mine + prior_weight * old_mine) / (counts_mine[:, :, None] + prior_weight)
    return (new_codebook, row_error)


def solution(mesh):
    in_specs = (
        P(("list", "rep"), None),
        P(("list", "rep"), None),
        P(("list", "rep")),
        P(("list", "rep"), None),
        P(("list", "rep")),
        P("list", None),
        P(),
    )
    out_specs = (P("rep", None, None), P(("list", "rep")))
    return jax.shard_map(body, mesh=mesh, in_specs=in_specs, out_specs=out_specs, check_vma=False)
```

profile of v0, /device:TPU:2, one launch (start us, length us, event | category | flops | bytes accessed | tf_op | source)
XLA Modules:
  0.0 582.1 jit_solution(2420515403371690203)
XLA Ops:
  7.8 0.7 fusion.22
  8.5 0.6 reduce-window.6
  9.3 0.9 fusion.19
  10.2 0.7 compare_select_fusion.2
  10.9 1.6 scatter_custom_fusion.1
  12.5 0.7 all_to_all.17
  13.1 7.6 %all-to-all-start.1 = ((s32[32,1,32]{2,1,0:T(1,128)}), s32[32,1,32]{2,1,0:T(1,128)S(1)}, u32[]{:S(2)}, u32[]{:S(2)}) async-start(s32[32,1,32]{2,1,0:T(1,128)} %all_to_all.17), calls=%async_computation.1 | async-start | bytes 32768 | tf_op jit(solution)/shard_map/all_to_all | solution.py:72
  20.8 0.8 copy.39
  21.6 1.3 scatter_custom_fusion
  23.1 0.8 reshape.243
  23.9 3.1 all-to-all-done.1
  26.9 5.0 all-to-all-start
  31.9 3.7 scatter_custom_fusion.2
  35.6 2.7 all-to-all-done
  38.3 5.8 %all-to-all-start.2 = ((bf16[32,32,1024]{2,1,0:T(8,128)(2,1)}), bf16[32,32,1024]{2,1,0:T(8,128)(2,1)}, u32[]{:S(2)}, u32[]{:S(2)}) async-start(bf16[32,32,1024]{2,1,0:T(8,128)(2,1)} %bitcast.13), calls=%async_computation.2 | async-start | bytes 4194304 | tf_op jit(solution)/shard_map/all_to_all | solution.py:65
  44.4 0.6 copy.49
  45.2 8.8 %gather_fusion = bf16[1024,1024]{1,0:T(8,128)(2,1)} fusion(bf16[2048,1024]{1,0:T(8,128)(2,1)} %param.14, s32[1024]{0:T(1024)S(1)} %broadcast_clamp_fusion.1), kind=kCustom, calls=%fused_computation | custom fusion | bytes 4198400 | tf_op jit(solution)/shard_map/gather | solution.py:87
  53.9 4.1 copy.44
  58.0 4.0 convert_element_type.53
  62.0 8.1 %copy.45 = f32[1024,16,64]{2,1,0:T(8,128)} copy(f32[1024,16,64]{0,2,1:T(8,128)} %bitcast.73) | data formatting | bytes 8388608 | tf_op jit(solution)/shard_map/convert_element_type | solution.py:87
  70.2 0.5 broadcast.194
  70.7 0.8 reduce.8
  72.4 176.0 %gather_fusion.1 = f32[16384,64]{1,0:T(8,128)} fusion(f32[16,256,64]{2,1,0:T(8,128)S(1)} %copy.49, s32[16384]{0:T(1024)S(1)} %reshape.188), kind=kCustom, calls=%fused_computation.1 | custom fusion | bytes 8519680 | tf_op jit(solution)/shard_map/gather | solution.py:15
  248.5 7.6 %gather.13 = f32[32,32,1024]{2,1,0:T(8,128)} reshape(f32[16384,64]{1,0:T(8,128)} %gather_fusion.1) | data formatting | bytes 8388608 | tf_op jit(solution)/shard_map/gather | solution.py:15
  256.1 6.9 %reshape.177 = f32[1024,16,64]{2,1,0:T(8,128)} reshape(bf16[32,32,1024]{2,1,0:T(8,128)(2,1)} %all-to-all-done.2) | data formatting | bytes 6291456 | tf_op jit(solution)/shard_map/convert_element_type | solution.py:88
  262.9 7.7 %fusion.9 = bf16[16,1024,64]{2,0,1:T(8,128)(2,1)S(1)} fusion(f32[1024,16,64]{2,1,0:T(8,128)} %reshape.177, f32[1024,16,64]{2,1,0:T(8,128)} %copy.45, pred[1024]{0:T(1024)(128)(4,1)S(1)} %ge.17), kind=kLoop, calls=%fused_computation.19 | loop fusion | flops 3145728 | bytes 10486784 | tf_op jit(solution)/shard_map/transpose | solution.py:20
  270.6 3.0 copy.46
  273.6 40.9 %while.12 = (s32[]{:T(128)}, f32[16,256,64]{1,2,0:T(8,128)}, f32[16,256]{1,0:T(8,128)S(1)}, s32[16,1024]{1,0:T(8,128)S(1)}, pred[1024]{0:T(1024)(128)(4,1)S(1)},...) while((s32[]{:T(128)}, f32[16,256,64]{1,2,0:T(8,128)}, f32[16,256]{1,0:T(8,128)S(1)}, ...), condition=%wide.region_8.9_spmd, body=%wide.region_6.8_spmd.sunk | while | flops 35389184 | bytes 350301 | solution.py:35
  273.6 2.1 fusion.31
  276.2 2.1 fusion.31
  278.8 2.1 fusion.31
  281.3 2.1 fusion.31
  283.4 0.3 convert_reduce_fusion.2
  283.9 2.1 fusion.31
  286.0 0.3 convert_reduce_fusion.2
  286.4 2.1 fusion.31
  288.6 0.3 convert_reduce_fusion.2
  289.0 2.1 fusion.31
  291.1 0.3 convert_reduce_fusion.2
  291.5 2.1 fusion.31
  293.7 0.3 convert_reduce_fusion.2
  294.1 2.1 fusion.31
  296.2 0.3 convert_reduce_fusion.2
  296.6 2.1 fusion.31
  299.2 2.1 fusion.31
  301.3 0.3 convert_reduce_fusion.2
  301.8 2.1 fusion.31
  303.9 0.3 convert_reduce_fusion.2
  304.3 2.1 fusion.31
  306.9 2.1 fusion.31
  309.0 0.3 convert_reduce_fusion.2
  309.4 2.1 fusion.31
  311.6 0.3 convert_reduce_fusion.2
  312.0 2.1 fusion.31
  314.6 5.1 multiply_reduce_fusion
  319.6 0.6 bitcast_select_fusion
  320.3 7.4 %all-to-all-start.3 = ((f32[32,1,32]{2,1,0:T(1,128)}), f32[32,1,32]{2,1,0:T(1,128)S(1)}, u32[]{:S(2)}, u32[]{:S(2)}) async-start(f32[32,1,32]{2,1,0:T(1,128)} %bitcast.21), calls=%async_computation.3 | async-start | bytes 32768 | tf_op jit(solution)/shard_map/all_to_all | solution.py:90
  327.7 79.8 %psum.15 = f32[16,256]{1,0:T(8,128)S(1)} all-reduce(f32[16,256]{1,0:T(8,128)S(1)} %get-tuple-element.36), channel_id=1, replica_groups=mesh['list'=32,'rep'=8] {'list','rep'}, use_global_device_ids=true, to_apply=%region_10.11 | all-reduce | flops 4096 | bytes 32768 | tf_op jit(solution)/shard_map/psum | solution.py:98
  407.5 0.5 broadcast.188
  408.0 0.7 reduce.7
  408.8 1.4 gather_fusion.2
  410.1 0.6 broadcast_select_fusion
  410.7 162.9 %all-reduce.2.cloned.1.call-done = f32[16,256,64]{1,2,0:T(8,128)} async-done(((f32[16,256,64]{1,2,0:T(8,128)}), f32[16,256,64]{1,2,0:T(8,128)}) %all-reduce.2.cloned.1.call-update) | async-done | bytes 1048592 | tf_op jit(solution)/shard_map/psum | solution.py:98
  573.6 1.6 add_divide_fusion
  (70 shorter events, 4.8 us)
Async XLA Ops:
  9.1 35.3 %copy-start = (f32[16,256,64]{1,2,0:T(8,128)S(1)}, f32[16,256,64]{1,2,0:T(8,128)}, u32[]{:S(2)}) copy-start(f32[16,256,64]{1,2,0:T(8,128)} %param.15) | copy-start | bytes 3145732
  13.1 13.8 %all-to-all-start.1 = ((s32[32,1,32]{2,1,0:T(1,128)}), s32[32,1,32]{2,1,0:T(1,128)S(1)}, u32[]{:S(2)}, u32[]{:S(2)}) async-start(s32[32,1,32]{2,1,0:T(1,128)} %all_to_all.17), calls=%async_computation.1 | async-start | bytes 32768 | tf_op jit(solution)/shard_map/all_to_all | solution.py:72
  26.9 11.4 %all-to-all-start = ((s32[32,1,512]{2,1,0:T(1,128)}), s32[32,1,512]{2,1,0:T(1,128)S(1)}, u32[]{:S(2)}, u32[]{:S(2)}) async-start(s32[32,1,512]{2,1,0:T(1,128)} %reshape.243), calls=%async_computation | async-start | bytes 131072 | tf_op jit(solution)/shard_map/all_to_all | solution.py:75
  38.3 217.7 %all-to-all-start.2 = ((bf16[32,32,1024]{2,1,0:T(8,128)(2,1)}), bf16[32,32,1024]{2,1,0:T(8,128)(2,1)}, u32[]{:S(2)}, u32[]{:S(2)}) async-start(bf16[32,32,1024]{2,1,0:T(8,128)(2,1)} %bitcast.13), calls=%async_computation.2 | async-start | bytes 4194304 | tf_op jit(solution)/shard_map/all_to_all | solution.py:65
  44.2 529.5 %all-reduce.2.cloned.1.call-start = ((), (), s32[]{:S(2)}) async-start(), calls=%async_computation.4 | async-start | bytes 2097152 | tf_op jit(solution)/shard_map/psum | solution.py:98
  320.3 87.2 %all-to-all-start.3 = ((f32[32,1,32]{2,1,0:T(1,128)}), f32[32,1,32]{2,1,0:T(1,128)S(1)}, u32[]{:S(2)}, u32[]{:S(2)}) async-start(f32[32,1,32]{2,1,0:T(1,128)} %bitcast.21), calls=%async_computation.3 | async-start | bytes 32768 | tf_op jit(solution)/shard_map/all_to_all | solution.py:90
Sparse Core Ops, SparseCore 0:
  314.7 258.9 all-reduce.1
where the time goes:
time: 584 us; the launch traced here: 582 us
  local copies, waits for them, and re-layouts  229 us (39%)
  waiting for transfers between devices  169 us (29%)
  blocking collectives  79.8 us (14%)
  matrix products  34 us (6%)
  other arithmetic  29.6 us (5%)
  starting transfers between devices  26.1 us (4%)
  between operations  14.9 us (3%)
    gather x2, local copies, waits for them, and re-layouts, code_statistics(): codebook[jnp.arange(subspaces)[None, :], pq_codes]  184 us
    psum x1, waiting for transfers between devices, body(): sums_all, counts_all = lax.psum((sums, counts), ('list', 'rep'))  163 us
    psum x1, blocking collectives, body(): sums_all, counts_all = lax.psum((sums, counts), ('list', 'rep'))  79.8 us
    dot_general x16, matrix products, per_subspace(): lax.dot_general(onehot, part_rows, (((0,), (0,)), ((), ())), preferred_el...  34 us
    convert_element_type x2, local copies, waits for them, and re-layouts, body(): centroids[jnp.clip(got_slot, 0, list_count - 1)].astype(jnp.float32)  12.2 us
  transfers between devices with their start and end apart: 5, of which 3 were waited for; matrix products, arithmetic and copies ran while one was open for 39% of the time, Pallas kernels for 0%

commit v1 on v0

--- a/solution.py
+++ b/solution.py
@@ -95,7 +95,7 @@
     replicas = lax.axis_size("rep")
     share = subspaces // replicas
     first_sub = lax.axis_index("rep") * share
-    sums_all, counts_all = lax.psum((sums, counts), ("list", "rep"))
+    sums_all, counts_all = lax.psum(lax.psum((sums, counts), "list"), "rep")
     sums_mine = lax.dynamic_slice_in_dim(sums_all, first_sub, share, 0)
     counts_mine = lax.dynamic_slice_in_dim(counts_all, first_sub, share, 0)
     old_mine = lax.dynamic_slice_in_dim(codebook, first_sub, share, 0)

time: 584 us -> 502 us (0.86)
  the two profiles are of different devices: /device:TPU:2 before, /device:TPU:0 now
where the time goes in v1:
time: 502 us; the launch traced here: 501 us
  local copies, waits for them, and re-layouts  229 us (46%)
  blocking collectives  161 us (32%)
  matrix products  34 us (7%)
  other arithmetic  29.7 us (6%)
  starting transfers between devices  18.3 us (4%)
  between operations  14.9 us (3%)
  waiting for transfers between devices  13.2 us (3%)
    gather x2, local copies, waits for them, and re-layouts, code_statistics(): codebook[jnp.arange(subspaces)[None, :], pq_codes]  184 us
    psum x2, blocking collectives, body(): sums_all, counts_all = lax.psum(lax.psum((sums, counts), 'list'), 'rep')  161 us
    dot_general x16, matrix products, per_subspace(): lax.dot_general(onehot, part_rows, (((0,), (0,)), ((), ())), preferred_el...  34 us
    convert_element_type x2, local copies, waits for them, and re-layouts, body(): centroids[jnp.clip(got_slot, 0, list_count - 1)].astype(jnp.float32)  12.2 us
  transfers between devices with their start and end apart: 6, of which 3 were waited for; matrix products, arithmetic and copies ran while one was open for 45% of the time, Pallas kernels for 0%

profile of v1, /device:TPU:0, one launch (start us, length us, event | category | flops | bytes accessed | tf_op | source)
XLA Modules:
  0.0 500.6 jit_solution(5048934553795387928)
XLA Ops:
  7.8 0.7 fusion.22
  8.5 0.6 reduce-window.6
  9.3 0.9 fusion.19
  10.2 0.7 compare_select_fusion.2
  10.9 1.6 scatter_custom_fusion.1
  12.5 0.7 all_to_all.17
  13.1 5.6 %all-to-all-start.1 = ((s32[32,1,32]{2,1,0:T(1,128)}), s32[32,1,32]{2,1,0:T(1,128)S(1)}, u32[]{:S(2)}, u32[]{:S(2)}) async-start(s32[32,1,32]{2,1,0:T(1,128)} %all_to_all.17), calls=%async_computation.1 | async-start | bytes 32768 | tf_op jit(solution)/shard_map/all_to_all | solution.py:72
  18.7 0.8 copy.39
  19.5 1.3 scatter_custom_fusion
  21.0 0.8 reshape.243
  21.8 4.3 all-to-all-done.1
  26.1 3.9 all-to-all-start
  30.0 3.8 scatter_custom_fusion.2
  33.7 3.7 all-to-all-done
  37.5 4.8 all-to-all-start.2
  42.5 0.6 copy.49
  43.2 8.8 %gather_fusion = bf16[1024,1024]{1,0:T(8,128)(2,1)} fusion(bf16[2048,1024]{1,0:T(8,128)(2,1)} %param.14, s32[1024]{0:T(1024)S(1)} %broadcast_clamp_fusion.1), kind=kCustom, calls=%fused_computation | custom fusion | bytes 4198400 | tf_op jit(solution)/shard_map/gather | solution.py:87
  52.0 4.1 copy.44
  56.1 8.1 %copy.45 = f32[1024,16,64]{2,1,0:T(8,128)} copy(f32[1024,16,64]{0,2,1:T(8,128)} %bitcast.73) | data formatting | bytes 8388608 | tf_op jit(solution)/shard_map/convert_element_type | solution.py:87
  64.3 0.5 broadcast.194
  64.8 0.8 reduce.8
  66.0 5.1 %all-to-all-done.2 = bf16[32,32,1024]{2,1,0:T(8,128)(2,1)} async-done(((bf16[32,32,1024]{2,1,0:T(8,128)(2,1)}), bf16[32,32,1024]{2,1,0:T(8,128)(2,1)}, u32[]{:S(2)}, u32[]{:S(2)}) %all-to-all-start.2) | async-done | bytes 2097184 | tf_op jit(solution)/shard_map/all_to_all | solution.py:65
  71.1 6.9 %reshape.177 = f32[1024,16,64]{2,1,0:T(8,128)} reshape(bf16[32,32,1024]{2,1,0:T(8,128)(2,1)} %all-to-all-done.2) | data formatting | bytes 6291456 | tf_op jit(solution)/shard_map/convert_element_type | solution.py:88
  78.0 7.7 %fusion.9 = bf16[16,1024,64]{2,0,1:T(8,128)(2,1)S(1)} fusion(f32[1024,16,64]{2,1,0:T(8,128)} %reshape.177, f32[1024,16,64]{2,1,0:T(8,128)} %copy.45, pred[1024]{0:T(1024)(128)(4,1)S(1)} %ge.17), kind=kLoop, calls=%fused_computation.19 | loop fusion | flops 3145728 | bytes 10486784 | tf_op jit(solution)/shard_map/transpose | solution.py:20
  85.7 3.0 copy.46
  88.7 40.9 %while.12 = (s32[]{:T(128)}, f32[16,256,64]{1,2,0:T(8,128)}, f32[16,256]{1,0:T(8,128)S(1)}, s32[16,1024]{1,0:T(8,128)S(1)}, pred[1024]{0:T(1024)(128)(4,1)S(1)},...) while((s32[]{:T(128)}, f32[16,256,64]{1,2,0:T(8,128)}, f32[16,256]{1,0:T(8,128)S(1)}, ...), condition=%wide.region_8.9_spmd, body=%wide.region_6.8_spmd.sunk | while | flops 35389184 | bytes 350301 | solution.py:35
  88.7 2.1 fusion.31
  90.8 0.3 convert_reduce_fusion.2
  91.2 2.1 fusion.31
  93.4 0.3 convert_reduce_fusion.2
  93.8 2.1 fusion.31
  95.9 0.3 convert_reduce_fusion.2
  96.4 2.1 fusion.31
  98.5 0.3 convert_reduce_fusion.2
  98.9 2.1 fusion.31
  101.0 0.3 convert_reduce_fusion.2
  101.5 2.1 fusion.31
  104.0 2.1 fusion.31
  106.2 0.3 convert_reduce_fusion.2
  106.6 2.1 fusion.31
  108.7 0.3 convert_reduce_fusion.2
  109.1 2.1 fusion.31
  111.3 0.3 convert_reduce_fusion.2
  111.7 2.1 fusion.31
  114.2 2.1 fusion.31
  116.8 2.1 fusion.31
  119.4 2.1 fusion.31
  121.9 2.1 fusion.31
  124.5 2.1 fusion.31
  127.0 2.1 fusion.31
  129.1 0.4 convert_reduce_fusion.2
  129.6 4.0 convert_element_type.53
  134.2 176.0 %gather_fusion.1 = f32[16384,64]{1,0:T(8,128)} fusion(f32[16,256,64]{2,1,0:T(8,128)S(1)} %copy.49, s32[16384]{0:T(1024)S(1)} %reshape.188), kind=kCustom, calls=%fused_computation.1 | custom fusion | bytes 8519680 | tf_op jit(solution)/shard_map/gather | solution.py:15
  310.3 7.6 %gather.13 = f32[32,32,1024]{2,1,0:T(8,128)} reshape(f32[16384,64]{1,0:T(8,128)} %gather_fusion.1) | data formatting | bytes 8388608 | tf_op jit(solution)/shard_map/gather | solution.py:15
  317.9 5.1 %multiply_reduce_fusion = f32[32,32]{1,0:T(8,128)S(1)} fusion(f32[32,32,1024]{2,1,0:T(8,128)} %gather.13, f32[32,32,1024]{2,1,0:T(8,128)} %bitcast.74, pred[32,32]{1,0:T(8,128)(4,1)S(1)} %fusion.25, bf16[32,32,1024]{2,1,0:T(8,128)(2,1)} %all-to-all-done.2), kind=kLoop, calls=%fused_computation.20 | loop fusion | flops 6290432 | bytes 10490880 | tf_op jit(solution)/shard_map/reduce_sum | solution.py:18
  323.0 0.6 bitcast_select_fusion
  323.6 3.8 all-to-all-start.3
  327.5 128.7 %psum.30 = f32[16,256]{1,0:T(8,128)S(1)} all-reduce(f32[16,256]{1,0:T(8,128)S(1)} %get-tuple-element.36), channel_id=1, replica_groups=mesh['list'=32,'rep'=8] {'list'}, use_global_device_ids=true, to_apply=%region_11.12 | all-reduce | flops 4096 | bytes 32768 | tf_op jit(solution)/shard_map/psum | solution.py:98
  456.1 32.7 %psum.31 = f32[16,256]{1,0:T(8,128)S(1)} all-reduce(f32[16,256]{1,0:T(8,128)S(1)} %psum.30), channel_id=1, replica_groups=mesh['list'=32,'rep'=8] {'rep'}, use_global_device_ids=true, to_apply=%region_12.13 | all-reduce | flops 4096 | bytes 32768 | tf_op jit(solution)/shard_map/psum | solution.py:98
  488.9 0.5 broadcast.188
  489.4 0.7 reduce.7
  490.2 1.4 gather_fusion.2
  491.5 0.6 broadcast_select_fusion
  492.1 1.6 add_divide_fusion
  (74 shorter events, 5.2 us)
Async XLA Ops:
  9.1 33.4 %copy-start = (f32[16,256,64]{1,2,0:T(8,128)S(1)}, f32[16,256,64]{1,2,0:T(8,128)}, u32[]{:S(2)}) copy-start(f32[16,256,64]{1,2,0:T(8,128)} %param.15) | copy-start | bytes 3145732
  13.1 13.0 %all-to-all-start.1 = ((s32[32,1,32]{2,1,0:T(1,128)}), s32[32,1,32]{2,1,0:T(1,128)S(1)}, u32[]{:S(2)}, u32[]{:S(2)}) async-start(s32[32,1,32]{2,1,0:T(1,128)} %all_to_all.17), calls=%async_computation.1 | async-start | bytes 32768 | tf_op jit(solution)/shard_map/all_to_all | solution.py:72
  26.1 11.4 %all-to-all-start = ((s32[32,1,512]{2,1,0:T(1,128)}), s32[32,1,512]{2,1,0:T(1,128)S(1)}, u32[]{:S(2)}, u32[]{:S(2)}) async-start(s32[32,1,512]{2,1,0:T(1,128)} %reshape.243), calls=%async_computation | async-start | bytes 131072 | tf_op jit(solution)/shard_map/all_to_all | solution.py:75
  37.5 33.6 %all-to-all-start.2 = ((bf16[32,32,1024]{2,1,0:T(8,128)(2,1)}), bf16[32,32,1024]{2,1,0:T(8,128)(2,1)}, u32[]{:S(2)}, u32[]{:S(2)}) async-start(bf16[32,32,1024]{2,1,0:T(8,128)(2,1)} %bitcast.13), calls=%async_computation.2 | async-start | bytes 4194304 | tf_op jit(solution)/shard_map/all_to_all | solution.py:65
  42.3 275.6 %all-reduce.3.cloned.1.call-start = ((), (), s32[]{:S(2)}) async-start(), calls=%async_computation.4 | async-start | bytes 2097152 | tf_op jit(solution)/shard_map/psum | solution.py:98
  129.6 362.5 %all-reduce.5.cloned.1.call-start = ((), (), s32[]{:S(2)}) async-start(), calls=%async_computation.5 | async-start | bytes 2097152 | tf_op jit(solution)/shard_map/psum | solution.py:98
  323.6 165.3 %all-to-all-start.3 = ((f32[32,1,32]{2,1,0:T(1,128)}), f32[32,1,32]{2,1,0:T(1,128)S(1)}, u32[]{:S(2)}, u32[]{:S(2)}) async-start(f32[32,1,32]{2,1,0:T(1,128)} %bitcast.21), calls=%async_computation.3 | async-start | bytes 32768 | tf_op jit(solution)/shard_map/all_to_all | solution.py:90
Sparse Core Ops, SparseCore 0:
  129.7 113.7 all-reduce.2
  318.0 75.0 all-reduce.4
